TPU v7x, 32 devices: a whole 2x2x4 slice. The times are simulated.
32 devices in a mesh: wide: 8 (over y, x, core), narrow: 4 (over z).
Axes of the slice: x: 2, y: 2, z: 4, core: 2. Of those that a mesh axis runs over, the one named last changes fastest.
Arguments:
- tokens: bfloat16 [10240, 2048], P(('wide', 'narrow')), may hold values from -6 to 6
- cotangent: bfloat16 [10240, 2048], P(('wide', 'narrow')), may hold values from -6 to 6
- lengths: int32 [32], P(('wide', 'narrow')), may hold values from 40 to 320, as said below
- positions: int32 [10240], P(('wide', 'narrow')), may hold values from 0 to 319, as said below
- norm_attn: bfloat16 [2048], P(('wide', 'narrow')), may hold values from 0.25 to 1.75
- w_query: bfloat16 [2048, 2048], P(('wide', 'narrow')), may hold values from -0.1875 to 0.1875
- w_key: bfloat16 [2048, 256], P(('wide', 'narrow')), may hold values from -0.1875 to 0.1875
- w_value: bfloat16 [2048, 256], P(('wide', 'narrow')), may hold values from -0.125 to 0.125
- w_output: bfloat16 [2048, 2048], P(('wide', 'narrow')), may hold values from -0.5 to 0.5
- norm_mlp: bfloat16 [2048], P(('wide', 'narrow')), may hold values from 0.25 to 1.75
- w_gate: bfloat16 [2048, 5632], P(('wide', 'narrow')), may hold values from -0.125 to 0.125
- w_up: bfloat16 [2048, 5632], P(('wide', 'narrow')), may hold values from -0.125 to 0.125
- w_down: bfloat16 [2048, 5632], P(('wide', 'narrow')), may hold values from -0.109375 to 0.109375
Outputs:
- output: bfloat16 [10240, 2048], P(('wide', 'narrow'))
- grad_tokens: float32 [10240, 2048], P(('wide', 'narrow'))
- grad_norm_attn: float32 [2048], P(('wide', 'narrow'))
- grad_w_query: float32 [2048, 2048], P(('wide', 'narrow'))
- grad_w_key: float32 [2048, 256], P(('wide', 'narrow'))
- grad_w_value: float32 [2048, 256], P(('wide', 'narrow'))
- grad_w_output: float32 [2048, 2048], P(('wide', 'narrow'))
- grad_norm_mlp: float32 [2048], P(('wide', 'narrow'))
- grad_w_gate: float32 [2048, 5632], P(('wide', 'narrow'))
- grad_w_up: float32 [2048, 5632], P(('wide', 'narrow'))
- grad_w_down: float32 [2048, 5632], P(('wide', 'narrow'))
Inputs may be any that keep to these rules, and one draw needn't show every extreme that they name: `lengths`: one sequence of every draw uses all 320 slots. Within a sequence positions rise by one from slot to slot and restart at 0 where a packed document starts; every sequence starts at position 0, and the first sequence holds a single document.
All inputs are finite; a program needn't handle non-finite values.
Results may differ from a plain program's by a relative error of at most 0.014.
The roundings to bfloat16 on the way count: a program that leaves them out, or rounds other values in their place, can miss the bound.
Values may be sent and summed in bfloat16 or wider, within the bound.
A program may use at most 384 MiB of HBM per device.

v0:
```python
import math
import jax
import jax.numpy as jnp
from jax import lax
from jax.sharding import PartitionSpec as P

QUERY_HEADS = 32
KEY_VALUE_HEADS = 4
HEAD_SIZE = 64
norm_eps = 1e-05
rope_base = 10000.0
masked_score = -1e30
contract_last = (((1,), (1,)), ((), ()))
contract_first = (((0,), (0,)), ((), ()))


def rope_tables(positions):
    half_dim = HEAD_SIZE // 2
    inv_freq = jnp.exp(
        -math.log(rope_base) * jnp.arange(half_dim, dtype=jnp.float32) * 2.0 / HEAD_SIZE
    )
    angles = positions.astype(jnp.float32)[..., None] * inv_freq
    cosine = jnp.cos(angles)
    sine_part = jnp.sin(angles)
    return (jnp.concatenate([cosine, cosine], -1), jnp.concatenate([sine_part, sine_part], -1))


def apply_rotary(values, cosine_table, sine_table):
    half_dim = values.shape[-1] // 2
    turned = jnp.concatenate([-values[..., half_dim:], values[..., :half_dim]], -1)
    return values * cosine_table[..., None, :] + turned * sine_table[..., None, :]


def invert_rotary(grad_rows, cosine_table, sine_table):
    half_dim = grad_rows.shape[-1] // 2
    with_cos = grad_rows * cosine_table[..., None, :]
    with_sin = grad_rows * sine_table[..., None, :]
    return with_cos + jnp.concatenate([with_sin[..., half_dim:], -with_sin[..., :half_dim]], -1)


def normalize(values):
    return values * lax.rsqrt(jnp.mean(values * values, axis=-1, keepdims=True) + norm_eps)


def norm_back(grad_hat, normed, values):
    row_scale = lax.rsqrt(jnp.mean(values * values, axis=-1, keepdims=True) + norm_eps)
    return row_scale * (grad_hat - normed * jnp.mean(grad_hat * normed, axis=-1, keepdims=True))


def attention_inputs(normed, norm_attn, w_query, w_key, w_value):
    gain_piece = lax.all_gather(norm_attn, ("wide", "narrow"), axis=0, tiled=True)
    query_rows = lax.all_gather(w_query, ("wide", "narrow"), axis=0, tiled=True)
    key_rows = lax.all_gather(w_key, ("wide", "narrow"), axis=0, tiled=True)
    value_rows = lax.all_gather(w_value, ("wide", "narrow"), axis=0, tiled=True)
    gain_float = gain_piece.astype(jnp.float32)
    columns = (normed * gain_float).astype(jnp.bfloat16)
    query_sum = jnp.dot(columns, query_rows, preferred_element_type=jnp.float32)
    key_sum = jnp.dot(columns, key_rows, preferred_element_type=jnp.float32)
    value_sum = jnp.dot(columns, value_rows, preferred_element_type=jnp.float32)
    return (gain_float, columns, query_sum, key_sum, value_sum)


def mlp_inputs(normed, norm_mlp, w_gate, w_up):
    gain_piece = lax.all_gather(norm_mlp, ("wide", "narrow"), axis=0, tiled=True)
    gate_rows = lax.all_gather(w_gate, ("wide", "narrow"), axis=0, tiled=True)
    up_rows = lax.all_gather(w_up, ("wide", "narrow"), axis=0, tiled=True)
    gain_float = gain_piece.astype(jnp.float32)
    columns = (normed * gain_float).astype(jnp.bfloat16)
    gate_sum = jnp.dot(columns, gate_rows, preferred_element_type=jnp.float32)
    up_sum = jnp.dot(columns, up_rows, preferred_element_type=jnp.float32)
    return (gain_float, columns, gate_sum, up_sum)


def head_slices(query_rotated, key_rotated, value_reduced, shared_key_head):
    row_total_count = query_rotated.shape[0]
    heads_per_group = QUERY_HEADS // KEY_VALUE_HEADS
    query_head = query_rotated[
        :,
        shared_key_head
        * heads_per_group
        * HEAD_SIZE : (shared_key_head + 1)
        * heads_per_group
        * HEAD_SIZE,
    ].reshape(row_total_count, heads_per_group, HEAD_SIZE)
    key_head = key_rotated[:, shared_key_head * HEAD_SIZE : (shared_key_head + 1) * HEAD_SIZE]
    value_head = value_reduced[:, shared_key_head * HEAD_SIZE : (shared_key_head + 1) * HEAD_SIZE]
    return (query_head, key_head, value_head)


def head_scores(query_head, key_head):
    row_total_count = query_head.shape[0]
    causal = jnp.arange(row_total_count)[:, None] >= jnp.arange(row_total_count)[None, :]
    raw_scores = jnp.einsum("qrd,kd->rqk", query_head, key_head, preferred_element_type=jnp.float32)
    return jnp.where(causal, raw_scores * HEAD_SIZE ** (-0.5), masked_score)


def attend(query_rotated, key_rotated, value_reduced):
    row_total_count = query_rotated.shape[0]
    heads_per_group = QUERY_HEADS // KEY_VALUE_HEADS
    contexts = []
    log_totals = []
    for shared_key_head in range(KEY_VALUE_HEADS):
        query_head, key_head, value_head = head_slices(
            query_rotated, key_rotated, value_reduced, shared_key_head
        )
        scores = head_scores(query_head, key_head)
        row_peak = jnp.max(scores, axis=-1, keepdims=True)
        exp_scores = jnp.exp(scores - row_peak)
        row_total = jnp.sum(exp_scores, axis=-1, keepdims=True)
        probs = exp_scores / row_total
        context_head = jnp.einsum(
            "rqk,kd->qrd",
            probs.astype(jnp.bfloat16),
            value_head,
            preferred_element_type=jnp.float32,
        )
        contexts.append(context_head.reshape(row_total_count, heads_per_group * HEAD_SIZE))
        log_totals.append(row_peak + jnp.log(row_total))
    return (jnp.concatenate(contexts, 1).astype(jnp.bfloat16), log_totals)


def attend_back(query_rotated, key_rotated, value_reduced, log_totals, grad_context):
    row_total_count = query_rotated.shape[0]
    heads_per_group = QUERY_HEADS // KEY_VALUE_HEADS
    score_scale = HEAD_SIZE ** (-0.5)
    query_grads = []
    key_grads = []
    value_grads = []
    for shared_key_head in range(KEY_VALUE_HEADS):
        query_head, key_head, value_head = head_slices(
            query_rotated, key_rotated, value_reduced, shared_key_head
        )
        scores = head_scores(query_head, key_head)
        probs = jnp.exp(scores - log_totals[shared_key_head])
        probs_low = probs.astype(jnp.bfloat16)
        grad_head = grad_context[
            :,
            shared_key_head
            * heads_per_group
            * HEAD_SIZE : (shared_key_head + 1)
            * heads_per_group
            * HEAD_SIZE,
        ].reshape(row_total_count, heads_per_group, HEAD_SIZE)
        grad_probs = jnp.einsum(
            "qrd,kd->rqk", grad_head, value_head, preferred_element_type=jnp.float32
        )
        value_grads.append(
            jnp.einsum("rqk,qrd->kd", probs_low, grad_head, preferred_element_type=jnp.float32)
        )
        inner_sum = jnp.sum(grad_probs * probs, axis=-1, keepdims=True)
        grad_scores = (probs * (grad_probs - inner_sum) * score_scale).astype(jnp.bfloat16)
        query_grad = jnp.einsum(
            "rqk,kd->qrd", grad_scores, key_head, preferred_element_type=jnp.float32
        )
        query_grads.append(query_grad.reshape(row_total_count, heads_per_group * HEAD_SIZE))
        key_grads.append(
            jnp.einsum("rqk,qrd->kd", grad_scores, query_head, preferred_element_type=jnp.float32)
        )
    return (
        jnp.concatenate(query_grads, 1),
        jnp.concatenate(key_grads, 1),
        jnp.concatenate(value_grads, 1),
    )


def make_term(width_sides, other_sides):
    down_side, mlp_side, attn_side, qkv_side = width_sides
    mixed_rows, gate_rows, up_rows, context_rows, query_rows, key_rows, value_rows = other_sides

    def grad_term(first_row, row_span):
        pieces = [
            lax.dot_general(
                down_side, mixed_rows, contract_first, preferred_element_type=jnp.float32
            ),
            lax.dot_general(
                mlp_side, gate_rows, contract_first, preferred_element_type=jnp.float32
            ),
            lax.dot_general(mlp_side, up_rows, contract_first, preferred_element_type=jnp.float32),
            lax.dot_general(
                attn_side, context_rows, contract_first, preferred_element_type=jnp.float32
            ),
            lax.dot_general(
                qkv_side, query_rows, contract_first, preferred_element_type=jnp.float32
            ),
            lax.dot_general(qkv_side, key_rows, contract_first, preferred_element_type=jnp.float32),
            lax.dot_general(
                qkv_side, value_rows, contract_first, preferred_element_type=jnp.float32
            ),
        ]
        return jnp.concatenate(pieces, 1)

    return grad_term


def per_device(
    tokens,
    cotangent,
    lengths,
    positions,
    norm_attn,
    w_query,
    w_key,
    w_value,
    w_output,
    norm_mlp,
    w_gate,
    w_up,
    w_down,
):
    row_total_count = tokens.shape[0]
    shard_rows = w_query.shape[0]
    query_width = w_query.shape[1]
    key_width = w_key.shape[1]
    hidden_width = w_gate.shape[1]
    inputs = tokens.astype(jnp.float32)
    valid_rows = (jnp.arange(row_total_count) < lengths[0]).astype(jnp.float32)[:, None]
    cosine_table, sine_table = rope_tables(positions)
    normed_attn = normalize(inputs)
    gain_attn_full, scaled_attn, query_pre, key_unrotated, value_pre = attention_inputs(
        normed_attn, norm_attn, w_query, w_key, w_value
    )
    query_rotated = (
        apply_rotary(
            query_pre.reshape(row_total_count, QUERY_HEADS, HEAD_SIZE), cosine_table, sine_table
        )
        .reshape(row_total_count, query_width)
        .astype(jnp.bfloat16)
    )
    key_rotated = (
        apply_rotary(
            key_unrotated.reshape(row_total_count, KEY_VALUE_HEADS, HEAD_SIZE),
            cosine_table,
            sine_table,
        )
        .reshape(row_total_count, key_width)
        .astype(jnp.bfloat16)
    )
    value_reduced = value_pre.astype(jnp.bfloat16)
    context, log_totals = attend(query_rotated, key_rotated, value_reduced)
    attn_out = lax.dot_general(
        context,
        lax.all_gather(w_output, ("wide", "narrow"), axis=0, tiled=True),
        contract_last,
        preferred_element_type=jnp.float32,
    )
    hidden = inputs + attn_out
    normed_mlp = normalize(hidden)
    gain_mlp_full, scaled_mlp, gate_proj, up_proj = mlp_inputs(normed_mlp, norm_mlp, w_gate, w_up)
    mixed_low = (gate_proj * jax.nn.sigmoid(gate_proj) * up_proj).astype(jnp.bfloat16)
    mlp_out = lax.dot_general(
        mixed_low,
        lax.all_gather(w_down, ("wide", "narrow"), axis=0, tiled=True),
        contract_last,
        preferred_element_type=jnp.float32,
    )
    output = (valid_rows * (hidden + mlp_out)).astype(jnp.bfloat16)
    grad_y = cotangent.astype(jnp.float32) * valid_rows
    grad_y_low = grad_y.astype(jnp.bfloat16)
    grad_cols = grad_y_low
    grad_mixed = jnp.dot(
        grad_cols,
        lax.all_gather(w_down, ("wide", "narrow"), axis=0, tiled=True),
        preferred_element_type=jnp.float32,
    )
    again_values = mlp_inputs(normed_mlp, norm_mlp, w_gate, w_up)
    gate_proj = again_values[2]
    up_proj = again_values[3]
    sigmoid_gate = jax.nn.sigmoid(gate_proj)
    grad_gate = (
        grad_mixed * up_proj * (sigmoid_gate * (1.0 + gate_proj * (1.0 - sigmoid_gate)))
    ).astype(jnp.bfloat16)
    grad_up = (grad_mixed * (gate_proj * sigmoid_gate)).astype(jnp.bfloat16)
    gate_rows = lax.all_gather(w_gate, ("wide", "narrow"), axis=0, tiled=True)
    up_rows = lax.all_gather(w_up, ("wide", "narrow"), axis=0, tiled=True)
    columns = lax.dot_general(
        grad_gate, gate_rows, contract_last, preferred_element_type=jnp.float32
    )
    columns = columns + lax.dot_general(
        grad_up, up_rows, contract_last, preferred_element_type=jnp.float32
    )
    grad_xn2 = columns
    grad_gain_mlp = jnp.sum(grad_xn2 * normed_mlp, axis=0)
    grad_hidden = grad_y + norm_back(grad_xn2 * gain_mlp_full, normed_mlp, hidden)
    grad_attn_low = grad_hidden.astype(jnp.bfloat16)
    grad_cols = grad_attn_low
    grad_context = jnp.dot(
        grad_cols,
        lax.all_gather(w_output, ("wide", "narrow"), axis=0, tiled=True),
        preferred_element_type=jnp.float32,
    )
    grad_context = grad_context.astype(jnp.bfloat16)
    grad_query_rot, gradient_key_rotated, grad_value_sum = attend_back(
        query_rotated, key_rotated, value_reduced, log_totals, grad_context
    )
    grad_query = (
        invert_rotary(
            grad_query_rot.reshape(row_total_count, QUERY_HEADS, HEAD_SIZE),
            cosine_table,
            sine_table,
        )
        .reshape(row_total_count, query_width)
        .astype(jnp.bfloat16)
    )
    grad_key = (
        invert_rotary(
            gradient_key_rotated.reshape(row_total_count, KEY_VALUE_HEADS, HEAD_SIZE),
            cosine_table,
            sine_table,
        )
        .reshape(row_total_count, key_width)
        .astype(jnp.bfloat16)
    )
    grad_value = grad_value_sum.astype(jnp.bfloat16)
    query_rows = lax.all_gather(w_query, ("wide", "narrow"), axis=0, tiled=True)
    key_rows = lax.all_gather(w_key, ("wide", "narrow"), axis=0, tiled=True)
    value_rows = lax.all_gather(w_value, ("wide", "narrow"), axis=0, tiled=True)
    columns = lax.dot_general(
        grad_query, query_rows, contract_last, preferred_element_type=jnp.float32
    )
    columns = columns + lax.dot_general(
        grad_key, key_rows, contract_last, preferred_element_type=jnp.float32
    )
    columns = columns + lax.dot_general(
        grad_value, value_rows, contract_last, preferred_element_type=jnp.float32
    )
    local_term = make_term(
        (grad_y_low, scaled_mlp, grad_attn_low, scaled_attn),
        (mixed_low, grad_gate, grad_up, context, grad_query, grad_key, grad_value),
    )
    all_sums = lax.psum_scatter(
        local_term(jnp.int32(0), lax.axis_size(("wide", "narrow")) * shard_rows),
        ("wide", "narrow"),
        scatter_dimension=0,
        tiled=True,
    )
    edges = [0]
    for width in (
        hidden_width,
        hidden_width,
        hidden_width,
        query_width,
        query_width,
        key_width,
        key_width,
    ):
        edges.append(edges[-1] + width)
    grad_w_down = all_sums[:, edges[0] : edges[1]]
    grad_w_gate = all_sums[:, edges[1] : edges[2]]
    grad_w_up = all_sums[:, edges[2] : edges[3]]
    grad_w_output = all_sums[:, edges[3] : edges[4]]
    grad_w_query = all_sums[:, edges[4] : edges[5]]
    grad_w_key = all_sums[:, edges[5] : edges[6]]
    grad_w_value = all_sums[:, edges[6] : edges[7]]
    grad_gain_attn = jnp.sum(columns * normed_attn, axis=0)
    grad_tokens = grad_hidden + norm_back(columns * gain_attn_full, normed_attn, inputs)
    grad_norm_attn, grad_norm_mlp = (
        lax.psum_scatter(grad_gain_attn, ("wide", "narrow"), scatter_dimension=0, tiled=True),
        lax.psum_scatter(grad_gain_mlp, ("wide", "narrow"), scatter_dimension=0, tiled=True),
    )
    return (
        output,
        grad_tokens,
        grad_norm_attn,
        grad_w_query,
        grad_w_key,
        grad_w_value,
        grad_w_output,
        grad_norm_mlp,
        grad_w_gate,
        grad_w_up,
        grad_w_down,
    )


def solution(mesh):
    in_specs = (
        P(("wide", "narrow"), None),
        P(("wide", "narrow"), None),
        P(("wide", "narrow")),
        P(("wide", "narrow")),
        P(("wide", "narrow")),
        P(("wide", "narrow"), None),
        P(("wide", "narrow"), None),
        P(("wide", "narrow"), None),
        P(("wide", "narrow"), None),
        P(("wide", "narrow")),
        P(("wide", "narrow"), None),
        P(("wide", "narrow"), None),
        P(("wide", "narrow"), None),
    )
    out_specs = (
        P(("wide", "narrow"), None),
        P(("wide", "narrow"), None),
        P(("wide", "narrow")),
        P(("wide", "narrow"), None),
        P(("wide", "narrow"), None),
        P(("wide", "narrow"), None),
        P(("wide", "narrow"), None),
        P(("wide", "narrow")),
        P(("wide", "narrow"), None),
        P(("wide", "narrow"), None),
        P(("wide", "narrow"), None),
    )
    return jax.shard_map(
        per_device, mesh=mesh, in_specs=in_specs, out_specs=out_specs, check_vma=False
    )
```

profile of v0, /device:TPU:0, one launch (start us, length us, event | category | flops | bytes accessed | tf_op | source)
XLA Modules:
  0.0 2423.2 jit_solution(7380186025434072481)
XLA Ops:
  15.0 42.1 %all-reduce.5 = (bf16[2048]{0:T(1024)(128)(2,1)S(1)}, bf16[2048]{0:T(1024)(128)(2,1)S(1)}) all-reduce(bf16[2048]{0:T(1024)(128)(2,1)S(1)} %dynamic-update-slice, bf16[2048]{0:T(1024)(128)(2,1)S(1)} %dynamic-update-slice.1), channel_id=1, replica_groups=mesh['wide'=8,'narrow'=4] {'wide','narrow'}, use_global_device_ids=true, to_apply=%add | all-reduce | flops 4096 | bytes 16384
  69.8 53.6 %all-gather.8.cloned.1.call-done = bf16[2048,256]{1,0:T(8,128)(2,1)} async-done(((bf16[64,256]{1,0:T(8,128)(2,1)}), bf16[2048,256]{1,0:T(8,128)(2,1)}) %all-gather.8.cloned.1.call-update) | async-done | bytes 1048592 | tf_op jit(solution)/shard_map/all_gather | solution.py:54
  125.8 76.9 %all-gather.12.cloned.1.call-done = bf16[2048,2048]{1,0:T(8,128)(2,1)} async-done(((bf16[64,2048]{1,0:T(8,128)(2,1)}), bf16[2048,2048]{1,0:T(8,128)(2,1)}) %all-gather.12.cloned.1.call-update) | async-done | bytes 8388624 | tf_op jit(solution)/shard_map/all_gather | solution.py:52
  202.7 7.8 fusion.144
  238.2 43.3 %all-gather.14.cloned.1.call-done = bf16[2048,2048]{1,0:T(8,128)(2,1)} async-done(((bf16[64,2048]{1,0:T(8,128)(2,1)}), bf16[2048,2048]{1,0:T(8,128)(2,1)}) %all-gather.14.cloned.1.call-update) | async-done | bytes 8388624 | tf_op jit(solution)/shard_map/all_gather | solution.py:242
  281.5 7.5 multiply_reduce_fusion.2
  291.4 136.0 %all-gather.18.cloned.1.call-done = bf16[2048,5632]{1,0:T(8,128)(2,1)} async-done(((bf16[64,5632]{1,0:T(8,128)(2,1)}), bf16[2048,5632]{1,0:T(8,128)(2,1)}) %all-gather.18.cloned.1.call-update) | async-done | bytes 23068688 | tf_op jit(solution)/shard_map/all_gather | solution.py:66
  427.4 14.9 fusion.161
  442.3 130.6 %all-gather.16.cloned.1.call-done = bf16[2048,5632]{1,0:T(8,128)(2,1)} async-done(((bf16[64,5632]{1,0:T(8,128)(2,1)}), bf16[2048,5632]{1,0:T(8,128)(2,1)}) %all-gather.16.cloned.1.call-update) | async-done | bytes 23068688 | tf_op jit(solution)/shard_map/all_gather | solution.py:65
  572.9 14.9 fusion.160
  587.8 130.7 %all-gather.20.cloned.1.call-done = bf16[2048,5632]{1,0:T(8,128)(2,1)} async-done(((bf16[64,5632]{1,0:T(8,128)(2,1)}), bf16[2048,5632]{1,0:T(8,128)(2,1)}) %all-gather.20.cloned.1.call-update) | async-done | bytes 23068688 | tf_op jit(solution)/shard_map/all_gather | solution.py:252
  718.6 20.5 multiply_convert_fusion
  739.0 14.3 fusion.162
  753.4 15.6 multiply_reduce_fusion
  772.8 6.2 convolution_convert_fusion
  785.7 7.3 fusion.83
  793.0 8.2 fusion.75
  807.1 8.2 fusion.84
  815.3 8.7 fusion.76
  830.0 8.0 fusion.85
  838.0 8.3 fusion.77
  852.3 8.0 fusion.82
  860.3 8.2 fusion.74
  874.9 23.4 convolution_dynamic-update-slice_fusion.2
  898.3 23.2 convolution_dynamic-update-slice_fusion.1
  921.4 20.5 convolution_dynamic-update-slice_fusion
  942.0 9.8 convolution_dynamic-update-slice_fusion.4
  955.1 8.6 convolution_dynamic-update-slice_fusion.3
  968.3 7.0 fusion.163
  980.2 38.6 %all-reduce.4 = (f32[2048]{0:T(1024)S(1)}, f32[2048]{0:T(1024)S(1)}) all-reduce(f32[2048]{0:T(1024)S(1)} %get-tuple-element.13, f32[2048]{0:T(1024)S(1)} %copy-done.66), channel_id=2, replica_groups=mesh['wide'=8,'narrow'=4] {'wide','narrow'}, use_global_device_ids=true, to_apply=%region_17.18.clone | all-reduce | flops 4096 | bytes 32768
  1025.0 19.3 fusion.31
  1044.3 1363.6 %reduce-scatter.2.cloned.1.call-done = f32[64,21504]{1,0:T(8,128)} async-done(((f32[2048,21504]{1,0:T(8,128)}), f32[64,21504]{1,0:T(8,128)}) %reduce-scatter.2.cloned.1.call-update) | async-done | bytes 5505040 | tf_op jit(solution)/shard_map/reduce_scatter | solution.py:330
  (240 shorter events, 113.3 us)
Async XLA Ops:
  7.2 60.4 %all-gather.10.cloned.1.call-start = ((), (), s32[]{:S(2)}) async-start(), calls=%async_computation.2 | async-start | bytes 1081344 | tf_op jit(solution)/shard_map/all_gather | solution.py:53
  7.9 115.4 %all-gather.8.cloned.1.call-start = ((), (), s32[]{:S(2)}) async-start(), calls=%async_computation.1 | async-start | bytes 1081344 | tf_op jit(solution)/shard_map/all_gather | solution.py:54
  8.7 194.0 %all-gather.12.cloned.1.call-start = ((), (), s32[]{:S(2)}) async-start(), calls=%async_computation.3 | async-start | bytes 8650752 | tf_op jit(solution)/shard_map/all_gather | solution.py:52
  9.4 272.1 %all-gather.14.cloned.1.call-start = ((), (), s32[]{:S(2)}) async-start(), calls=%async_computation.4 | async-start | bytes 8650752 | tf_op jit(solution)/shard_map/all_gather | solution.py:242
  10.0 417.4 %all-gather.18.cloned.1.call-start = ((), (), s32[]{:S(2)}) async-start(), calls=%async_computation.6 | async-start | bytes 23789568 | tf_op jit(solution)/shard_map/all_gather | solution.py:66
  10.6 562.3 %all-gather.16.cloned.1.call-start = ((), (), s32[]{:S(2)}) async-start(), calls=%async_computation.5 | async-start | bytes 23789568 | tf_op jit(solution)/shard_map/all_gather | solution.py:65
  11.1 707.4 %all-gather.20.cloned.1.call-start = ((), (), s32[]{:S(2)}) async-start(), calls=%async_computation.7 | async-start | bytes 23789568 | tf_op jit(solution)/shard_map/all_gather | solution.py:252
  11.9 2396.0 %reduce-scatter.2.cloned.1.call-start = ((), (), s32[]{:S(2)}) async-start(), calls=%async_computation.8 | async-start | bytes 181665792 | tf_op jit(solution)/shard_map/reduce_scatter | solution.py:330
  57.1 145.6 %copy-start.55 = (f32[2048]{0:T(1024)}, f32[2048]{0:T(1024)S(1)}, u32[]{:S(2)}) copy-start(f32[2048]{0:T(1024)S(1)} %convert_element_type.106) | copy-start | bytes 24580
  62.9 706.1 %copy-start.57 = (f32[320]{0:T(512)}, f32[320]{0:T(512)S(1)}, u32[]{:S(2)}) copy-start(f32[320]{0:T(512)S(1)} %fusion.120) | copy-start | bytes 3844
  63.0 153.2 %copy-start.22 = (f32[320,64]{0,1:T(8,128)}, f32[320,64]{0,1:T(8,128)S(1)}, u32[]{:S(2)}) copy-start(f32[320,64]{0,1:T(8,128)S(1)} %pad_maximum_fusion.9) | copy-start | bytes 245764
  63.4 139.3 %copy-start.59 = (f32[320]{0:T(512)}, f32[320]{0:T(512)S(1)}, u32[]{:S(2)}) copy-start(f32[320]{0:T(512)S(1)} %add_rsqrt_fusion.1) | copy-start | bytes 3844
  69.8 162.9 %copy-start.30 = (bf16[320,256]{1,0:T(8,128)(2,1)}, bf16[320,256]{1,0:T(8,128)(2,1)S(1)}, u32[]{:S(2)}) copy-start(bf16[320,256]{1,0:T(8,128)(2,1)S(1)} %add_convert_fusion.1) | copy-start | bytes 491524
  235.0 46.5 %copy-start.48 = (bf16[64,8,320]{2,0,1:T(8,128)(2,1)}, bf16[64,8,320]{2,0,1:T(8,128)(2,1)S(1)}, u32[]{:S(2)}) copy-start(bf16[64,8,320]{2,0,1:T(8,128)(2,1)S(1)} %fusion.80) | copy-start | bytes 983044
  235.8 45.7 %copy-start.50 = (bf16[64,8,320]{2,0,1:T(8,128)(2,1)}, bf16[64,8,320]{2,0,1:T(8,128)(2,1)S(1)}, u32[]{:S(2)}) copy-start(bf16[64,8,320]{2,0,1:T(8,128)(2,1)S(1)} %fusion.79) | copy-start | bytes 983044
  236.7 44.8 %copy-start.51 = (bf16[64,8,320]{2,0,1:T(8,128)(2,1)}, bf16[64,8,320]{2,0,1:T(8,128)(2,1)S(1)}, u32[]{:S(2)}) copy-start(bf16[64,8,320]{2,0,1:T(8,128)(2,1)S(1)} %fusion.78) | copy-start | bytes 983044
  289.1 495.8 %copy-start.64 = (f32[8,320]{1,0:T(8,128)}, f32[8,320]{1,0:T(8,128)S(1)}, u32[]{:S(2)}) copy-start(f32[8,320]{1,0:T(8,128)S(1)} %log_add_fusion.2) | copy-start | bytes 30724
  291.4 281.5 %copy-start.11 = (bf16[320,2048]{1,0:T(8,128)(2,1)}, bf16[320,2048]{1,0:T(8,128)(2,1)S(1)}, u32[]{:S(2)}) copy-start(bf16[320,2048]{1,0:T(8,128)(2,1)S(1)} %multiply_convert_fusion.3) | copy-start | bytes 3932164
  442.3 276.2 %copy-start.16 = (bf16[320,2048]{1,0:T(8,128)(2,1)S(1)}, bf16[320,2048]{1,0:T(8,128)(2,1)}, u32[]{:S(2)}) copy-start(bf16[320,2048]{1,0:T(8,128)(2,1)} %param.14) | copy-start | bytes 3932164
  739.0 14.3 copy-start.15
  815.3 8.7 copy-start.36
  838.0 8.4 copy-start.35
  860.2 8.4 copy-start.23
  860.3 8.5 copy-start.21
  898.3 23.2 copy-start.12
  921.4 20.5 copy-start.49
  942.0 9.8 copy-start.18
  942.0 9.8 copy-start.19
  955.0 8.6 copy-start.17
  955.0 10.9 copy-start.52
  955.0 10.9 copy-start.53
  955.0 10.9 copy-start.54
  (43 other events, 198.6 us)
Sparse Core Ops, SparseCore 0:
  11.0 56.4 all-gather.9
  70.5 52.8 all-gather.7
  126.3 76.3 all-gather.11
  205.5 75.9 all-gather.13
  284.2 143.1 all-gather.17
  430.1 142.7 all-gather.15
  575.7 142.7 all-gather.19
  968.4 1439.4 reduce-scatter.1
where the time goes:
time: 2430 us; the launch traced here: 2420 us
  waiting for transfers between devices  1940 us (80%)
  matrix products  319 us (13%)
  blocking collectives  80.7 us (3%)
  local copies, waits for them, and re-layouts  35.2 us (1%)
  other arithmetic  28.4 us (1%)
    reduce_scatter x1, waiting for transfers between devices, per_device(): lax.psum_scatter(local_term(jnp.int32(0), lax.axis_size(('wide', 'narrow'...  1360 us
    all_gather x1, waiting for transfers between devices, mlp_inputs(): up_rows = lax.all_gather(w_up, ('wide', 'narrow'), axis=0, tiled=True)  136 us
    all_gather x1, waiting for transfers between devices, per_device(): lax.all_gather(w_down, ('wide', 'narrow'), axis=0, tiled=True)  131 us
    all_gather x1, waiting for transfers between devices, mlp_inputs(): gate_rows = lax.all_gather(w_gate, ('wide', 'narrow'), axis=0, tiled=True)  131 us
    unnamed x2, blocking collectives  80.7 us
    all_gather x1, waiting for transfers between devices, attention_inputs(): query_rows = lax.all_gather(w_query, ('wide', 'narrow'), axis=0, tiled=True)  76.9 us
    all_gather x1, waiting for transfers between devices, attention_inputs(): value_rows = lax.all_gather(w_value, ('wide', 'narrow'), axis=0, tiled=True)  53.6 us
  transfers between devices with their start and end apart: 8, of which 8 were waited for; matrix products, arithmetic and copies ran while one was open for 5% of the time, Pallas kernels for 0%

commit v1 on v0

--- a/solution.py
+++ b/solution.py
@@ -50,8 +50,13 @@
 def attention_inputs(normed, norm_attn, w_query, w_key, w_value):
     gain_piece = lax.all_gather(norm_attn, ("wide", "narrow"), axis=0, tiled=True)
     query_rows = lax.all_gather(w_query, ("wide", "narrow"), axis=0, tiled=True)
-    key_rows = lax.all_gather(w_key, ("wide", "narrow"), axis=0, tiled=True)
-    value_rows = lax.all_gather(w_value, ("wide", "narrow"), axis=0, tiled=True)
+    key_rows, value_rows = jnp.split(
+        lax.all_gather(
+            jnp.concatenate([w_key, w_value], 1), ("wide", "narrow"), tiled=True, axis=0
+        ),
+        [w_key.shape[1]],
+        1,
+    )
     gain_float = gain_piece.astype(jnp.float32)
     columns = (normed * gain_float).astype(jnp.bfloat16)
     query_sum = jnp.dot(columns, query_rows, preferred_element_type=jnp.float32)

time: 2430 us -> 2380 us (0.979)
  waiting for transfers between devices: 1940 us -> 1880 us
    all_gather x2 -> x3, waiting for transfers between devices: 57.7 us -> 6.96 us  [the longest x1 6.95 us: attention_inputs(): lax.all_gather(jnp.concatenate([w_key, w_value], 1), ('wide', 'narrow'),...]
  transfers between devices with their start and end apart: 8 -> 9, of which waited for: 8 -> 7; matrix products, arithmetic and copies ran while one was open for 5% -> 16% of each run, Pallas kernels for 0% -> 0%
where the time goes in v1:
time: 2380 us; the launch traced here: 2370 us
  waiting for transfers between devices  1880 us (79%)
  matrix products  328 us (14%)
  blocking collectives  80.9 us (3%)
  local copies, waits for them, and re-layouts  38.7 us (2%)
  other arithmetic  31.4 us (1%)
    reduce_scatter x1, waiting for transfers between devices, per_device(): lax.psum_scatter(local_term(jnp.int32(0), lax.axis_size(('wide', 'narrow'...  1350 us
    all_gather x1, waiting for transfers between devices, mlp_inputs(): up_rows = lax.all_gather(w_up, ('wide', 'narrow'), axis=0, tiled=True)  137 us
    all_gather x1, waiting for transfers between devices, mlp_inputs(): gate_rows = lax.all_gather(w_gate, ('wide', 'narrow'), axis=0, tiled=True)  131 us
    all_gather x1, waiting for transfers between devices, per_device(): lax.all_gather(w_down, ('wide', 'narrow'), axis=0, tiled=True)  131 us
    unnamed x2, blocking collectives  80.9 us
    all_gather x1, waiting for transfers between devices, attention_inputs(): query_rows = lax.all_gather(w_query, ('wide', 'narrow'), axis=0, tiled=True)  74.4 us
  transfers between devices with their start and end apart: 9, of which 7 were waited for; matrix products, arithmetic and copies ran while one was open for 16% of the time, Pallas kernels for 0%

profile of v1, /device:TPU:0, one launch (start us, length us, event | category | flops | bytes accessed | tf_op | source)
XLA Modules:
  0.0 2374.3 jit_solution(12514624998021287632)
XLA Ops:
  15.9 42.1 %all-reduce.5 = (bf16[2048]{0:T(1024)(128)(2,1)S(1)}, bf16[2048]{0:T(1024)(128)(2,1)S(1)}) all-reduce(bf16[2048]{0:T(1024)(128)(2,1)S(1)} %dynamic-update-slice, bf16[2048]{0:T(1024)(128)(2,1)S(1)} %dynamic-update-slice.1), channel_id=1, replica_groups=mesh['wide'=8,'narrow'=4] {'wide','narrow'}, use_global_device_ids=true, to_apply=%add | all-reduce | flops 4096 | bytes 16384
  63.8 7.0 all-gather.9.cloned.1.call-done
  75.6 74.4 %all-gather.11.cloned.1.call-done = bf16[2048,2048]{1,0:T(8,128)(2,1)} async-done(((bf16[64,2048]{1,0:T(8,128)(2,1)}), bf16[2048,2048]{1,0:T(8,128)(2,1)}) %all-gather.11.cloned.1.call-update) | async-done | bytes 8388624 | tf_op jit(solution)/shard_map/all_gather | solution.py:52
  150.0 7.8 fusion.147
  187.7 41.3 %all-gather.13.cloned.1.call-done = bf16[2048,2048]{1,0:T(8,128)(2,1)} async-done(((bf16[64,2048]{1,0:T(8,128)(2,1)}), bf16[2048,2048]{1,0:T(8,128)(2,1)}) %all-gather.13.cloned.1.call-update) | async-done | bytes 8388624 | tf_op jit(solution)/shard_map/all_gather | solution.py:247
  228.9 7.3 multiply_reduce_fusion.2
  238.0 136.8 %all-gather.17.cloned.1.call-done = bf16[2048,5632]{1,0:T(8,128)(2,1)} async-done(((bf16[64,5632]{1,0:T(8,128)(2,1)}), bf16[2048,5632]{1,0:T(8,128)(2,1)}) %all-gather.17.cloned.1.call-update) | async-done | bytes 23068688 | tf_op jit(solution)/shard_map/all_gather | solution.py:71
  374.9 14.9 fusion.163
  389.8 130.6 %all-gather.15.cloned.1.call-done = bf16[2048,5632]{1,0:T(8,128)(2,1)} async-done(((bf16[64,5632]{1,0:T(8,128)(2,1)}), bf16[2048,5632]{1,0:T(8,128)(2,1)}) %all-gather.15.cloned.1.call-update) | async-done | bytes 23068688 | tf_op jit(solution)/shard_map/all_gather | solution.py:70
  520.4 14.9 fusion.162
  535.3 130.6 %all-gather.19.cloned.1.call-done = bf16[2048,5632]{1,0:T(8,128)(2,1)} async-done(((bf16[64,5632]{1,0:T(8,128)(2,1)}), bf16[2048,5632]{1,0:T(8,128)(2,1)}) %all-gather.19.cloned.1.call-update) | async-done | bytes 23068688 | tf_op jit(solution)/shard_map/all_gather | solution.py:257
  665.9 20.4 multiply_convert_fusion
  686.3 14.3 fusion.164
  700.6 15.8 multiply_reduce_fusion
  720.2 6.2 convolution_convert_fusion
  732.2 8.0 fusion.83
  740.2 8.3 fusion.75
  753.1 8.3 fusion.84
  761.4 8.4 fusion.76
  775.3 8.1 fusion.85
  783.4 8.2 fusion.77
  797.1 8.1 fusion.82
  805.2 8.3 fusion.74
  821.6 23.2 convolution_dynamic-update-slice_fusion.2
  844.8 23.0 convolution_dynamic-update-slice_fusion.1
  867.8 20.7 convolution_dynamic-update-slice_fusion
  888.6 10.0 convolution_dynamic-update-slice_fusion.4
  901.8 8.6 convolution_dynamic-update-slice_fusion.3
  920.4 9.2 fusion.165
  940.3 38.8 %all-reduce.4 = (f32[2048]{0:T(1024)S(1)}, f32[2048]{0:T(1024)S(1)}) all-reduce(f32[2048]{0:T(1024)S(1)} %get-tuple-element.13, f32[2048]{0:T(1024)S(1)} %copy-done.53), channel_id=2, replica_groups=mesh['wide'=8,'narrow'=4] {'wide','narrow'}, use_global_device_ids=true, to_apply=%region_17.18.clone | all-reduce | flops 4096 | bytes 32768
  985.4 19.3 fusion.31
  1004.7 1354.7 %reduce-scatter.2.cloned.1.call-done = f32[64,21504]{1,0:T(8,128)} async-done(((f32[2048,21504]{1,0:T(8,128)}), f32[64,21504]{1,0:T(8,128)}) %reduce-scatter.2.cloned.1.call-update) | async-done | bytes 5505040 | tf_op jit(solution)/shard_map/reduce_scatter | solution.py:335
  (222 shorter events, 121.1 us)
Async XLA Ops:
  7.2 63.6 %all-gather.9.cloned.1.call-start = ((), (), s32[]{:S(2)}) async-start(), calls=%async_computation.1 | async-start | bytes 2162688 | tf_op jit(solution)/shard_map/all_gather | solution.py:54
  8.8 141.2 %all-gather.11.cloned.1.call-start = ((), (), s32[]{:S(2)}) async-start(), calls=%async_computation.2 | async-start | bytes 8650752 | tf_op jit(solution)/shard_map/all_gather | solution.py:52
  9.5 219.4 %all-gather.13.cloned.1.call-start = ((), (), s32[]{:S(2)}) async-start(), calls=%async_computation.3 | async-start | bytes 8650752 | tf_op jit(solution)/shard_map/all_gather | solution.py:247
  10.3 364.6 %all-gather.17.cloned.1.call-start = ((), (), s32[]{:S(2)}) async-start(), calls=%async_computation.5 | async-start | bytes 23789568 | tf_op jit(solution)/shard_map/all_gather | solution.py:71
  10.8 509.5 %all-gather.15.cloned.1.call-start = ((), (), s32[]{:S(2)}) async-start(), calls=%async_computation.4 | async-start | bytes 23789568 | tf_op jit(solution)/shard_map/all_gather | solution.py:70
  11.4 654.4 %all-gather.19.cloned.1.call-start = ((), (), s32[]{:S(2)}) async-start(), calls=%async_computation.6 | async-start | bytes 23789568 | tf_op jit(solution)/shard_map/all_gather | solution.py:257
  12.0 917.6 %all-gather.21.cloned.1.call-start = ((), (), s32[]{:S(2)}) async-start(), calls=%async_computation.7 | async-start | bytes 1081344 | tf_op jit(solution)/shard_map/all_gather | solution.py:320
  12.8 921.7 %all-gather.23.cloned.1.call-start = ((), (), s32[]{:S(2)}) async-start(), calls=%async_computation.8 | async-start | bytes 1081344 | tf_op jit(solution)/shard_map/all_gather | solution.py:321
  13.5 2345.9 %reduce-scatter.2.cloned.1.call-start = ((), (), s32[]{:S(2)}) async-start(), calls=%async_computation.9 | async-start | bytes 181665792 | tf_op jit(solution)/shard_map/reduce_scatter | solution.py:335
  14.3 807.3 %copy-start.44 = (f32[320]{0:T(512)}, f32[320]{0:T(512)S(1)}, u32[]{:S(2)}) copy-start(f32[320]{0:T(512)S(1)} %fusion.123) | copy-start | bytes 3844
  15.3 134.6 %copy-start.46 = (f32[320]{0:T(512)}, f32[320]{0:T(512)S(1)}, u32[]{:S(2)}) copy-start(f32[320]{0:T(512)S(1)} %add_rsqrt_fusion.1) | copy-start | bytes 3844
  58.0 92.0 %copy-start.41 = (f32[2048]{0:T(1024)}, f32[2048]{0:T(1024)S(1)}, u32[]{:S(2)}) copy-start(f32[2048]{0:T(1024)S(1)} %convert_element_type.106) | copy-start | bytes 24580
  58.3 105.1 %copy-start.23 = (f32[320,64]{0,1:T(8,128)}, f32[320,64]{0,1:T(8,128)S(1)}, u32[]{:S(2)}) copy-start(f32[320,64]{0,1:T(8,128)S(1)} %pad_maximum_fusion.9) | copy-start | bytes 245764
  73.0 110.3 %copy-start.28 = (bf16[320,256]{1,0:T(8,128)(2,1)}, bf16[320,256]{1,0:T(8,128)(2,1)S(1)}, u32[]{:S(2)}) copy-start(bf16[320,256]{1,0:T(8,128)(2,1)S(1)} %add_convert_fusion.1) | copy-start | bytes 491524
  175.2 565.0 %copy-start.49 = (f32[8,320]{1,0:T(8,128)}, f32[8,320]{1,0:T(8,128)S(1)}, u32[]{:S(2)}) copy-start(f32[8,320]{1,0:T(8,128)S(1)} %log_add_fusion.2) | copy-start | bytes 30724
  178.2 583.2 %copy-start.51 = (f32[8,320]{1,0:T(8,128)}, f32[8,320]{1,0:T(8,128)S(1)}, u32[]{:S(2)}) copy-start(f32[8,320]{1,0:T(8,128)S(1)} %log_add_fusion.1) | copy-start | bytes 30724
  186.1 42.8 %copy-start.38 = (bf16[64,8,320]{2,0,1:T(8,128)(2,1)S(1)}, bf16[64,8,320]{2,0,1:T(8,128)(2,1)}, u32[]{:S(2)}) copy-start(bf16[64,8,320]{2,0,1:T(8,128)(2,1)} %fusion.80) | copy-start | bytes 983044
  186.1 42.8 %copy-start.39 = (bf16[64,8,320]{2,0,1:T(8,128)(2,1)S(1)}, bf16[64,8,320]{2,0,1:T(8,128)(2,1)}, u32[]{:S(2)}) copy-start(bf16[64,8,320]{2,0,1:T(8,128)(2,1)} %fusion.79) | copy-start | bytes 983044
  186.1 42.8 %copy-start.40 = (bf16[64,8,320]{2,0,1:T(8,128)(2,1)S(1)}, bf16[64,8,320]{2,0,1:T(8,128)(2,1)}, u32[]{:S(2)}) copy-start(bf16[64,8,320]{2,0,1:T(8,128)(2,1)} %fusion.78) | copy-start | bytes 983044
  238.0 282.3 %copy-start.10 = (bf16[320,2048]{1,0:T(8,128)(2,1)}, bf16[320,2048]{1,0:T(8,128)(2,1)S(1)}, u32[]{:S(2)}) copy-start(bf16[320,2048]{1,0:T(8,128)(2,1)S(1)} %multiply_convert_fusion.3) | copy-start | bytes 3932164
  389.8 276.1 %copy-start.15 = (bf16[320,2048]{1,0:T(8,128)(2,1)S(1)}, bf16[320,2048]{1,0:T(8,128)(2,1)}, u32[]{:S(2)}) copy-start(bf16[320,2048]{1,0:T(8,128)(2,1)} %param.14) | copy-start | bytes 3932164
  686.3 14.3 copy-start.14
  805.2 9.4 copy-start.24
  844.8 23.0 copy-start.11
  888.6 10.0 copy-start.17
  888.6 10.0 copy-start.18
  901.8 8.7 copy-start.32
  901.8 8.8 copy-start.34
  901.8 8.8 copy-start.35
  901.8 8.8 copy-start.36
  901.8 8.8 copy-start.37
  920.4 9.2 copy-start.30
  (33 other events, 117.5 us)
Sparse Core Ops, SparseCore 0:
  11.5 59.1 all-gather.8
  73.7 76.2 all-gather.10
  152.9 75.9 all-gather.12
  231.6 143.1 all-gather.16
  377.5 142.7 all-gather.14
  523.0 142.7 all-gather.18
  668.8 51.9 all-gather.20
  723.8 52.6 all-gather.22
  920.5 1438.8 reduce-scatter.1
